TPU v7x, 128 devices: a whole 4x4x4 slice. The times are simulated.
128 devices in a mesh: dp: 64 (over y, x_lo, z, core), tensor: 2 (over x_hi).
Axes of the slice: x: 4 (x_hi: 2, x_lo: 2; x = x_hi * 2 + x_lo), y: 4, z: 4, core: 2. Of those that a mesh axis runs over, the one named last changes fastest.
Arguments:
- tokens: bfloat16 [64, 512, 896], P(None, 'dp'), may hold values from -6 to 6
- cotangent: bfloat16 [64, 512, 896], P(None, 'dp'), may hold values from -6 to 6
- lengths: int32 [64], replicated, may hold values from 1 to 512, 24576 in all
- deal_order: int32 [64], replicated, may hold values from 0 to 63, each once
- gain_attn: bfloat16 [896], replicated, may hold values from 0.099609375 to 1.8984375
- w_query: bfloat16 [896, 896], P(None, 'tensor'), may hold values from -0.1875 to 0.1875
- b_query: bfloat16 [896], P('tensor'), may hold values from -3 to 3
- w_key: bfloat16 [896, 128], P(None, 'tensor'), may hold values from -0.1875 to 0.1875
- b_key: bfloat16 [128], P('tensor'), may hold values from -3 to 3
- w_value: bfloat16 [896, 128], P(None, 'tensor'), may hold values from -0.1875 to 0.1875
- b_value: bfloat16 [128], P('tensor'), may hold values from -3 to 3
- w_out: bfloat16 [896, 896], P('tensor'), may hold values from -1 to 1
- gain_mlp: bfloat16 [896], replicated, may hold values from 0.099609375 to 1.8984375
- w_gate: bfloat16 [896, 4864], P(None, 'tensor'), may hold values from -0.1875 to 0.1875
- w_up: bfloat16 [896, 4864], P(None, 'tensor'), may hold values from -0.1875 to 0.1875
- w_down: bfloat16 [4864, 896], P('tensor'), may hold values from -0.078125 to 0.078125
Outputs:
- layer_out: bfloat16 [64, 512, 896], P(None, 'dp')
- grad_tokens: bfloat16 [64, 512, 896], P(None, 'dp')
- grad_gain_attn: float32 [896], replicated
- grad_w_query: float32 [896, 896], P(None, 'tensor')
- grad_b_query: float32 [896], P('tensor')
- grad_w_key: float32 [896, 128], P(None, 'tensor')
- grad_b_key: float32 [128], P('tensor')
- grad_w_value: float32 [896, 128], P(None, 'tensor')
- grad_b_value: float32 [128], P('tensor')
- grad_w_out: float32 [896, 896], P('tensor')
- grad_gain_mlp: float32 [896], replicated
- grad_w_gate: float32 [896, 4864], P(None, 'tensor')
- grad_w_up: float32 [896, 4864], P(None, 'tensor')
- grad_w_down: float32 [4864, 896], P('tensor')
- rms_values: float32 [3], replicated
Inputs may be any that keep to these rules, and one draw needn't show every extreme that they name: Group g receives stored slot deal_order[g]; every slot goes to exactly one group. The first lengths[g] rows of the slot that group g receives are valid.
All inputs are finite; a program needn't handle non-finite values.
Results may differ from a plain program's by a relative error of at most 0.022.
Values may be sent and summed in bfloat16 or wider, within the bound.
A program may use at most 192 MiB of HBM per device.

v0:
```python
import math
import jax
import jax.numpy as jnp
from jax import lax
from jax.sharding import PartitionSpec as P

HD = 64
epsilon = 1e-06
rope_base = 1000000.0


def rope_tables(seq_rows, head_size):
    places = jnp.arange(seq_rows).astype(jnp.float32)
    frequency = rope_base ** (-jnp.arange(head_size // 2).astype(jnp.float32) * 2.0 / head_size)
    angles = places[:, None] * frequency[None, :]
    return (jnp.cos(angles)[:, None, :], jnp.sin(angles)[:, None, :])


def rotate(tensor, cos_table, sine_table):
    half_width = tensor.shape[-1] // 2
    first_half = tensor[..., :half_width]
    second_half = tensor[..., half_width:]
    return jnp.concatenate(
        [
            first_half * cos_table - second_half * sine_table,
            second_half * cos_table + first_half * sine_table,
        ],
        axis=-1,
    )


def unrotate(grad_rot, cos_table, sine_table):
    half_width = grad_rot.shape[-1] // 2
    first_half = grad_rot[..., :half_width]
    second_half = grad_rot[..., half_width:]
    return jnp.concatenate(
        [
            first_half * cos_table + second_half * sine_table,
            second_half * cos_table - first_half * sine_table,
        ],
        axis=-1,
    )


def dot_left(matrix, other):
    return lax.dot_general(
        matrix, other, (((0,), (0,)), ((), ())), preferred_element_type=jnp.float32
    )


def dot_right(matrix, other):
    return lax.dot_general(
        matrix, other, (((1,), (1,)), ((), ())), preferred_element_type=jnp.float32
    )


def on_device(
    tokens,
    cotangent,
    lengths,
    deal_order,
    gain_attn,
    w_query,
    b_query,
    w_key,
    b_key,
    w_value,
    b_value,
    w_out,
    gain_mlp,
    w_gate,
    w_up,
    w_down,
):
    restore = jnp.argsort(deal_order)
    arrived = (
        lax.all_to_all(tokens[deal_order], "dp", split_axis=0, concat_axis=1, tiled=True),
        lax.all_to_all(cotangent[deal_order], "dp", split_axis=0, concat_axis=1, tiled=True),
    )
    stream = arrived[0][0].astype(jnp.float32)
    grad_out = arrived[1][0].astype(jnp.float32)
    seq_rows, width = stream.shape
    head_size = HD
    length = lengths[lax.axis_index("dp")]
    places = jnp.arange(seq_rows)
    usable = places < length
    row_mask = usable[:, None]
    cos_table, sine_table = rope_tables(seq_rows, head_size)
    local_heads = w_query.shape[1] // head_size
    local_kv = w_key.shape[1] // head_size
    group_size = local_heads // local_kv
    score_scale = 1.0 / math.sqrt(head_size)
    allowed = (places[None, :] <= places[:, None]) & usable[None, :]
    gain_one = gain_attn.astype(jnp.float32)
    gain_two = gain_mlp.astype(jnp.float32)
    inverse_one = lax.rsqrt(jnp.mean(stream * stream, axis=-1, keepdims=True) + epsilon)
    normed = (stream * inverse_one * gain_one).astype(jnp.bfloat16)
    q_lin = jnp.dot(normed, w_query, preferred_element_type=jnp.float32) + b_query.astype(
        jnp.float32
    )
    k_lin = jnp.dot(normed, w_key, preferred_element_type=jnp.float32) + b_key.astype(jnp.float32)
    v_lin = jnp.dot(normed, w_value, preferred_element_type=jnp.float32) + b_value.astype(
        jnp.float32
    )
    queries = rotate(q_lin.reshape(seq_rows, local_heads, head_size), cos_table, sine_table).astype(
        jnp.bfloat16
    )
    queries = queries.reshape(seq_rows, local_kv, group_size, head_size)
    keys_rot = rotate(k_lin.reshape(seq_rows, local_kv, head_size), cos_table, sine_table).astype(
        jnp.bfloat16
    )
    values = v_lin.reshape(seq_rows, local_kv, head_size).astype(jnp.bfloat16)
    raw_scores = jnp.einsum("qkgd,pkd->kgqp", queries, keys_rot, preferred_element_type=jnp.float32)
    scores = jnp.where(allowed, raw_scores * score_scale, -1e30)
    top_score = jnp.max(scores, axis=-1, keepdims=True)
    expo = jnp.exp(scores - top_score)
    total = jnp.sum(expo, axis=-1, keepdims=True)
    log_total = top_score + jnp.log(total)
    probs_low = (expo / total).astype(jnp.bfloat16)
    mixed = jnp.einsum("kgqp,pkd->qkgd", probs_low, values, preferred_element_type=jnp.float32)
    mixed = mixed.reshape(seq_rows, local_heads * head_size).astype(jnp.bfloat16)
    attention = lax.psum(jnp.dot(mixed, w_out, preferred_element_type=jnp.float32), "tensor")
    residual = stream + attention
    inverse_two = lax.rsqrt(jnp.mean(residual * residual, axis=-1, keepdims=True) + epsilon)
    normed_two = (residual * inverse_two * gain_two).astype(jnp.bfloat16)
    gate_lin = jnp.dot(normed_two, w_gate, preferred_element_type=jnp.float32)
    up_lin = jnp.dot(normed_two, w_up, preferred_element_type=jnp.float32)
    sigmoid_gate = jax.nn.sigmoid(gate_lin)
    silu_gate = gate_lin * sigmoid_gate
    hidden = (silu_gate * up_lin).astype(jnp.bfloat16)
    mlp_branch = lax.psum(
        jnp.dot(hidden, w_down, preferred_element_type=jnp.float32).astype(jnp.bfloat16), "tensor"
    ).astype(jnp.float32)
    result = jnp.where(row_mask, residual + mlp_branch, 0.0)
    statistics = jnp.stack(
        [
            jnp.sum(result * result),
            jnp.sum(jnp.where(row_mask, attention * attention, 0.0)),
            jnp.sum(jnp.where(row_mask, mlp_branch * mlp_branch, 0.0)),
        ]
    )
    grad_y = jnp.where(row_mask, grad_out, 0.0)
    grad_low = grad_y.astype(jnp.bfloat16)
    grad_w_down = dot_left(hidden, grad_low)
    grad_hidden = dot_right(grad_low, w_down)
    grad_gate = (
        grad_hidden * up_lin * sigmoid_gate * (1.0 + gate_lin * (1.0 - sigmoid_gate))
    ).astype(jnp.bfloat16)
    grad_up = (grad_hidden * silu_gate).astype(jnp.bfloat16)
    grad_w_gate = dot_left(normed_two, grad_gate)
    grad_w_up = dot_left(normed_two, grad_up)
    grad_normed_two = lax.psum(dot_right(grad_gate, w_gate) + dot_right(grad_up, w_up), "tensor")
    grad_gain_mlp = jnp.sum(grad_normed_two * residual * inverse_two, axis=0)
    scaled_two = grad_normed_two * gain_two
    grad_resid = (
        grad_y
        + inverse_two * scaled_two
        - residual * inverse_two**3 * jnp.mean(scaled_two * residual, axis=-1, keepdims=True)
    )
    grad_attn = grad_resid.astype(jnp.bfloat16)
    grad_w_out = dot_left(mixed, grad_attn)
    grad_mixed = dot_right(grad_attn, w_out).astype(jnp.bfloat16)
    grad_mixed = grad_mixed.reshape(seq_rows, local_kv, group_size, head_size)
    probs = jnp.exp(scores - log_total)
    grad_probs = jnp.einsum(
        "qkgd,pkd->kgqp", grad_mixed, values, preferred_element_type=jnp.float32
    )
    grad_values = jnp.einsum(
        "kgqp,qkgd->pkd", probs_low, grad_mixed, preferred_element_type=jnp.float32
    )
    row_inner = jnp.sum(probs * grad_probs, axis=-1, keepdims=True)
    grad_scores = (probs * (grad_probs - row_inner) * score_scale).astype(jnp.bfloat16)
    grad_queries = jnp.einsum(
        "kgqp,pkd->qkgd", grad_scores, keys_rot, preferred_element_type=jnp.float32
    )
    grad_keys = jnp.einsum(
        "kgqp,qkgd->pkd", grad_scores, queries, preferred_element_type=jnp.float32
    )
    grad_q_lin = unrotate(
        grad_queries.reshape(seq_rows, local_heads, head_size), cos_table, sine_table
    )
    grad_q_lin = grad_q_lin.reshape(seq_rows, local_heads * head_size).astype(jnp.bfloat16)
    grad_k_lin = (
        unrotate(grad_keys, cos_table, sine_table)
        .reshape(seq_rows, local_kv * head_size)
        .astype(jnp.bfloat16)
    )
    grad_v_lin = grad_values.reshape(seq_rows, local_kv * head_size).astype(jnp.bfloat16)
    grad_w_query = dot_left(normed, grad_q_lin)
    grad_w_key = dot_left(normed, grad_k_lin)
    grad_w_value = dot_left(normed, grad_v_lin)
    grad_b_query = jnp.sum(grad_q_lin.astype(jnp.float32), axis=0)
    grad_b_key = jnp.sum(grad_k_lin.astype(jnp.float32), axis=0)
    grad_b_value = jnp.sum(grad_v_lin.astype(jnp.float32), axis=0)
    grad_normed = lax.psum(
        (
            dot_right(grad_q_lin, w_query)
            + dot_right(grad_k_lin, w_key)
            + dot_right(grad_v_lin, w_value)
        ).astype(jnp.bfloat16),
        "tensor",
    ).astype(jnp.float32)
    grad_gain_attn = jnp.sum(grad_normed * stream * inverse_one, axis=0)
    scaled_one = grad_normed * gain_one
    grad_stream = (
        grad_resid
        + inverse_one * scaled_one
        - stream * inverse_one**3 * jnp.mean(scaled_one * stream, axis=-1, keepdims=True)
    )
    (
        statistics,
        grad_gain_attn,
        grad_w_query,
        grad_b_query,
        grad_w_key,
        grad_b_key,
        grad_w_value,
        grad_b_value,
        grad_w_out,
        grad_gain_mlp,
        grad_w_gate,
        grad_w_up,
        grad_w_down,
    ) = lax.psum(
        (
            statistics,
            grad_gain_attn,
            grad_w_query,
            grad_b_query,
            grad_w_key,
            grad_b_key,
            grad_w_value,
            grad_b_value,
            grad_w_out,
            grad_gain_mlp,
            grad_w_gate,
            grad_w_up,
            grad_w_down,
        ),
        "dp",
    )
    sent_back = (
        lax.all_to_all(
            result.astype(jnp.bfloat16)[None], "dp", split_axis=1, concat_axis=0, tiled=True
        ),
        lax.all_to_all(
            grad_stream.astype(jnp.bfloat16)[None], "dp", split_axis=1, concat_axis=0, tiled=True
        ),
    )
    layer_out = sent_back[0][restore]
    grad_tokens = sent_back[1][restore]
    count = jnp.sum(lengths).astype(jnp.float32) * width
    rms_values = jnp.sqrt(statistics / count)
    return (
        layer_out,
        grad_tokens,
        grad_gain_attn,
        grad_w_query,
        grad_b_query,
        grad_w_key,
        grad_b_key,
        grad_w_value,
        grad_b_value,
        grad_w_out,
        grad_gain_mlp,
        grad_w_gate,
        grad_w_up,
        grad_w_down,
        rms_values,
    )


def solution(mesh):
    in_specs = (
        P(None, "dp", None),
        P(None, "dp", None),
        P(),
        P(),
        P(),
        P(None, "tensor"),
        P("tensor"),
        P(None, "tensor"),
        P("tensor"),
        P(None, "tensor"),
        P("tensor"),
        P("tensor", None),
        P(),
        P(None, "tensor"),
        P(None, "tensor"),
        P("tensor", None),
    )
    out_specs = (
        P(None, "dp", None),
        P(None, "dp", None),
        P(),
        P(None, "tensor"),
        P("tensor"),
        P(None, "tensor"),
        P("tensor"),
        P(None, "tensor"),
        P("tensor"),
        P("tensor", None),
        P(),
        P(None, "tensor"),
        P(None, "tensor"),
        P("tensor", None),
        P(),
    )
    return jax.shard_map(
        on_device, mesh=mesh, in_specs=in_specs, out_specs=out_specs, check_vma=False
    )
```

profile of v0, /device:TPU:0, one launch (start us, length us, event | category | flops | bytes accessed | tf_op | source)
XLA Modules:
  0.0 1022.6 jit_solution(5831000406995036942)
XLA Ops:
  8.4 1.6 gather_fusion
  10.0 10.1 all-to-all-start
  22.0 14.5 %all-to-all-done = bf16[64,8,896]{2,1,0:T(8,128)(2,1)S(1)} async-done(((bf16[64,8,896]{2,1,0:T(8,128)(2,1)}), bf16[64,8,896]{2,1,0:T(8,128)(2,1)S(1)}, u32[]{:S(2)}, u32[]{:S(2)}) %all-to-all-start) | async-done | bytes 917536 | tf_op jit(solution)/shard_map/all_to_all | solution.py:77
  37.7 0.8 convolution_add_fusion.1
  38.7 1.3 fusion.6
  40.0 1.5 fusion.4
  42.1 0.8 copy-done.2
  42.9 2.3 fusion.36
  45.2 0.7 copy-done.8
  46.0 2.0 fusion.103
  48.0 1.6 gather_fusion.2
  49.6 5.5 all-to-all-start.2
  55.3 65.8 %all-reduce.8.cloned.1.call-done = f32[512,896]{1,0:T(8,128)} async-done(((f32[512,896]{1,0:T(8,128)}), f32[512,896]{1,0:T(8,128)}) %all-reduce.8.cloned.1.call-update) | async-done | bytes 1835024 | tf_op jit(solution)/shard_map/psum | solution.py:122
  121.1 1.8 multiply_reduce_fusion.3
  124.5 7.2 fusion.104
  131.7 4.5 fusion.105
  136.2 10.4 %multiply_convert_fusion = (bf16[512,2432]{1,0:T(8,128)(2,1)}, bf16[512,2432]{1,0:T(8,128)(2,1)}, bf16[512,2432]{1,0:T(8,128)(2,1)S(1)}) fusion(f32[512,2432]{1,0:T(8,128)} %fusion.104, f32[512,2432]{1,0:T(8,128)} %fusion.105, bf16[2432,896]{1,0:T(8,128)(2,1)} %param.31, bf16[64,8,896]{2,1,0:T(8,128)(2,1)} %all-to-all-done.2, ...), kind=kOutput, calls=%fused_computation.15 | convolution fusion | flops 2251423744 | bytes 22708736 | tf_op jit(solution)/shard_map/dot_general | solution.py:52
  146.6 1.5 copy-done.61
  148.0 6.0 convolution_convert_fusion
  154.1 6.0 fusion.106
  160.1 6.4 convolution_add_fusion
  167.7 8.2 fusion.108
  176.0 6.1 fusion.109
  182.1 7.5 fusion.65
  189.6 9.3 all-reduce.10.cloned.1.call-done
  198.9 67.2 %all-reduce.12.cloned.1.call-done = f32[512,896]{1,0:T(8,128)} async-done(((f32[512,896]{1,0:T(8,128)}), f32[512,896]{1,0:T(8,128)}) %all-reduce.12.cloned.1.call-update) | async-done | bytes 1835024 | tf_op jit(solution)/shard_map/psum | solution.py:152
  266.2 5.5 select_reduce_fusion
  271.8 2.5 fusion.35
  275.2 2.4 fusion
  277.6 2.4 fusion.7
  280.0 0.7 convolution_bitcast_fusion
  280.8 1.2 convolution_bitcast_fusion.1
  282.1 2.3 convert_reduce_fusion.1
  284.7 0.8 copy-done.15
  287.0 1.4 add_convert_fusion
  288.7 1.1 fusion.61
  289.8 1.1 fusion.63
  291.0 1.9 fusion.59
  292.9 1.8 fusion.56
  294.7 3.8 copy.64
  299.1 8.1 reduce.8
  307.2 2.9 reshape.436
  310.1 8.4 all-to-all-start.1
  318.5 22.4 %all-reduce.14.cloned.1.call-done = bf16[512,896]{1,0:T(8,128)(2,1)} async-done(((bf16[512,896]{1,0:T(8,128)(2,1)}), bf16[512,896]{1,0:T(8,128)(2,1)}) %all-reduce.14.cloned.1.call-update) | async-done | bytes 917520 | tf_op jit(solution)/shard_map/psum | solution.py:195
  340.9 2.0 fusion.29
  343.0 1.7 fusion.55
  344.7 1.4 copy.63
  346.1 6.2 reduce.9
  352.4 1.3 reshape.438
  353.7 8.3 all-to-all-start.3
  362.7 2.0 sort.17
  365.6 2.1 pad_maximum_fusion.3
  367.6 5.4 reshape.437
  373.0 1.0 copy.62
  374.1 2.8 gather_fusion.1
  376.8 280.9 %all-reduce = (f32[896]{0:T(1024)}, f32[448]{0:T(512)}, f32[64]{0:T(128)}, f32[64]{0:T(128)}, f32[896]{0:T(1024)}, /*index=5*/f32[3]{0:T(128)S(1)}) all-reduce(f32[896]{0:T(1024)S(1)} %get-tuple-element.20, f32[448]{0:T(512)S(1)} %reduce_sum.145, f32[64]{0:T(128)S(1)} %convert_reduce_fusion.2, ...), channel_id=1, replica_groups=mesh['dp'=64,'tensor'=2] {'dp'}, use_global_device_ids=true, to_apply=%region_13.14 | all-reduce | flops 2371 | bytes 18968 | tf_op jit(solution)/shard_map/psum | solution.py:224
  659.1 1.6 gather_fusion.3
  660.7 331.3 %all-reduce.16.cloned.1.call-done = (f32[896,448]{0,1:T(8,128)}, f32[896,64]{0,1:T(8,128)}, f32[896,64]{0,1:T(8,128)}, f32[448,896]{1,0:T(8,128)}, f32[896,2432]...) async-done(((f32[896,448]{0,1:T(8,128)}, f32[896,64]{0,1:T(8,128)}, f32[896,64]{0,1:T(8,128)}, f32[448,896]{1,0:T(8,128)}, f32[896,2432]{1,0:T(8,128)}, ...) | async-done | bytes 29818896 | tf_op jit(solution)/shard_map/psum | solution.py:224
  992.0 2.8 copy.76
  996.2 1.2 copy.79
  997.4 8.6 copy.80
  1006.0 4.4 copy.81
  1010.4 1.6 slice-done.3
  1012.1 3.5 copy.82
  (199 shorter events, 15.1 us)
Async XLA Ops:
  7.2 12.9 %copy-start.56 = (bf16[64]{0:T(256)(128)(2,1)S(1)}, bf16[64]{0:T(256)(128)(2,1)}, u32[]{:S(2)}) copy-start(bf16[64]{0:T(256)(128)(2,1)} %param.26) | copy-start | bytes 388
  7.2 12.9 %copy-start.53 = (bf16[896]{0:T(1024)(128)(2,1)S(1)}, bf16[896]{0:T(1024)(128)(2,1)}, u32[]{:S(2)}) copy-start(bf16[896]{0:T(1024)(128)(2,1)} %param.20) | copy-start | bytes 5380
  7.2 13.0 %copy-start.55 = (bf16[448]{0:T(512)(128)(2,1)S(1)}, bf16[448]{0:T(512)(128)(2,1)}, u32[]{:S(2)}) copy-start(bf16[448]{0:T(512)(128)(2,1)} %param.22) | copy-start | bytes 2692
  7.2 13.0 %copy-start.57 = (bf16[64]{0:T(256)(128)(2,1)S(1)}, bf16[64]{0:T(256)(128)(2,1)}, u32[]{:S(2)}) copy-start(bf16[64]{0:T(256)(128)(2,1)} %param.24) | copy-start | bytes 388
  7.2 13.0 %copy-start.58 = (s32[64]{0:T(128)S(1)}, s32[64]{0:T(128)}, u32[]{:S(2)}) copy-start(s32[64]{0:T(128)} %param.18) | copy-start | bytes 772
  8.4 28.5 %copy-start.26 = (bf16[896,64]{0,1:T(8,128)(2,1)S(1)}, bf16[896,64]{0,1:T(8,128)(2,1)}, u32[]{:S(2)}) copy-start(bf16[896,64]{0,1:T(8,128)(2,1)} %param.23) | copy-start | bytes 344068
  10.0 27.7 %copy-start.14 = (bf16[896,448]{0,1:T(8,128)(2,1)S(1)}, bf16[896,448]{0,1:T(8,128)(2,1)}, u32[]{:S(2)}) copy-start(bf16[896,448]{0,1:T(8,128)(2,1)} %param.21) | copy-start | bytes 2408452
  10.0 26.5 %all-to-all-start = ((bf16[64,8,896]{2,1,0:T(8,128)(2,1)}), bf16[64,8,896]{2,1,0:T(8,128)(2,1)S(1)}, u32[]{:S(2)}, u32[]{:S(2)}) async-start(bf16[64,8,896]{2,1,0:T(8,128)(2,1)} %gather_fusion), calls=%async_computation | async-start | bytes 1835008 | tf_op jit(solution)/shard_map/all_to_all | solution.py:77
  20.1 101.1 %all-reduce.8.cloned.1.call-start = ((), (), s32[]{:S(2)}) async-start(), calls=%async_computation.4 | async-start | bytes 3670016 | tf_op jit(solution)/shard_map/psum | solution.py:122
  20.2 21.4 %copy-start.38 = (f32[896]{0:T(1024)}, f32[896]{0:T(1024)S(1)}, u32[]{:S(2)}) copy-start(f32[896]{0:T(1024)S(1)} %convert_element_type.242) | copy-start | bytes 10756
  20.8 17.7 %copy-start.48 = (f32[32]{0:T(128)}, f32[32]{0:T(128)S(1)}, u32[]{:S(2)}) copy-start(f32[32]{0:T(128)S(1)} %multiply_power_fusion) | copy-start | bytes 388
  21.5 114.7 %copy-start.50 = (pred[512]{0:T(512)(128)(4,1)}, pred[512]{0:T(512)(128)(4,1)S(1)}, u32[]{:S(2)}) copy-start(pred[512]{0:T(512)(128)(4,1)S(1)} %iota_compare_fusion.1) | copy-start | bytes 1540
  21.5 17.0 %copy-start.42 = (f32[512]{0:T(512)}, f32[512]{0:T(512)S(1)}, u32[]{:S(2)}) copy-start(f32[512]{0:T(512)S(1)} %iota_convert_fusion) | copy-start | bytes 6148
  21.8 16.7 %copy-start.16 = (f32[512,32]{0,1:T(8,128)}, f32[512,32]{0,1:T(8,128)S(1)}, u32[]{:S(2)}) copy-start(f32[512,32]{0,1:T(8,128)S(1)} %get-tuple-element.58) | copy-start | bytes 196612
  36.9 4.7 copy-start.44
  37.7 2.3 copy-start.22
  37.7 2.3 copy-start.24
  40.0 2.9 copy-start.2
  40.0 2.9 copy-start.34
  41.6 3.6 copy-start.36
  42.9 3.1 copy-start.6
  45.2 2.7 copy-start.11
  47.9 7.4 copy-start.54
  49.6 86.6 %all-to-all-start.2 = ((bf16[64,8,896]{2,1,0:T(8,128)(2,1)}), bf16[64,8,896]{2,1,0:T(8,128)(2,1)}, u32[]{:S(2)}, u32[]{:S(2)}) async-start(bf16[64,8,896]{2,1,0:T(8,128)(2,1)} %gather_fusion.2), calls=%async_computation.2 | async-start | bytes 1835008 | tf_op jit(solution)/shard_map/all_to_all | solution.py:78
  55.0 143.9 %all-reduce.10.cloned.1.call-start = ((), (), s32[]{:S(2)}) async-start(), calls=%async_computation.5 | async-start | bytes 1835008 | tf_op jit(solution)/shard_map/psum | solution.py:131
  55.3 69.1 %copy-start.32 = (f32[896]{0:T(1024)}, f32[896]{0:T(1024)S(1)}, u32[]{:S(2)}) copy-start(f32[896]{0:T(1024)S(1)} %convert_element_type.255) | copy-start | bytes 10756
  123.0 143.2 %copy-start.3 = (f32[512,896]{1,0:T(8,128)}, f32[512,896]{1,0:T(8,128)S(1)}, u32[]{:S(2)}) copy-start(f32[512,896]{1,0:T(8,128)S(1)} %get-tuple-element.40) | copy-start | bytes 5505028
  124.2 7.5 slice-start.5
  124.4 7.2 copy-start.12
  124.5 7.2 slice-start.6
  154.1 112.1 %all-reduce.12.cloned.1.call-start = ((), (), s32[]{:S(2)}) async-start(), calls=%async_computation.6 | async-start | bytes 3670016 | tf_op jit(solution)/shard_map/psum | solution.py:152
  154.1 6.0 copy-start.63
  166.5 174.5 %all-reduce.14.cloned.1.call-start = ((), (), s32[]{:S(2)}) async-start(), calls=%async_computation.7 | async-start | bytes 1835008 | tf_op jit(solution)/shard_map/psum | solution.py:195
  167.7 8.3 copy-start.13
  167.7 8.3 copy-start.64
  175.9 6.1 copy-start.51
  175.9 6.1 copy-start.62
  266.1 5.6 copy-start.5
  266.1 5.6 copy-start.33
  266.1 5.6 copy-start.41
  266.1 5.6 copy-start.47
  266.1 5.6 copy-start.52
  266.2 8.8 slice-start
  271.7 2.5 copy-start.7
  271.8 3.2 slice-start.1
  277.6 2.4 copy-start.23
  277.6 2.4 copy-start.25
  282.0 2.3 copy-start.17
  288.4 703.6 %all-reduce.16.cloned.1.call-start = ((), (), s32[]{:S(2)}) async-start(), calls=%async_computation.8 | async-start | bytes 59637760 | tf_op jit(solution)/shard_map/psum | solution.py:224
  289.8 3.0 copy-start.9
  307.2 11.3 %copy-start.45 = (f32[512]{0:T(512)S(1)}, f32[512]{0:T(512)}, u32[]{:S(2)}) copy-start(f32[512]{0:T(512)} %copy-done.44) | copy-start | bytes 6148
  310.1 43.6 %all-to-all-start.1 = ((bf16[64,2,3584]{2,1,0:T(2,128)(2,1)}), bf16[64,2,3584]{2,1,0:T(2,128)(2,1)}, u32[]{:S(2)}, u32[]{:S(2)}) async-start(bf16[64,2,3584]{2,1,0:T(2,128)(2,1)} %reshape.436), calls=%async_computation.1 | async-start | bytes 1835008 | tf_op jit(solution)/shard_map/all_to_all | solution.py:243
  352.4 9.6 copy-start.59
  352.4 10.3 %copy-start.60 = (s32[64]{0:T(128)S(1)}, s32[64]{0:T(128)}, u32[]{:S(2)}) copy-start(s32[64]{0:T(128)} %param.19) | copy-start | bytes 772
  353.7 304.6 %all-to-all-start.3 = ((bf16[64,2,3584]{2,1,0:T(2,128)(2,1)}), bf16[64,2,3584]{2,1,0:T(2,128)(2,1)S(1)}, u32[]{:S(2)}, u32[]{:S(2)}) async-start(bf16[64,2,3584]{2,1,0:T(2,128)(2,1)} %reshape.438), calls=%async_computation.3 | async-start | bytes 1835008 | tf_op jit(solution)/shard_map/all_to_all | solution.py:246
  373.0 3.8 copy-start.46
  992.0 2.8 copy-start.21
  992.0 3.5 copy-start.20
  992.0 4.2 copy-start.10
  997.4 8.6 copy-start.4
  997.4 13.0 %slice-start.2 = ((s8[8716288]{0:T(1024)(128)(4,1)}), s8[4194304]{0:T(1024)(128)(4,1)S(1)}, s32[]{:S(2)}) async-start(s8[8716288]{0:T(1024)(128)(4,1)} %bitcast.213), calls=%async_computation.11 | async-start | bytes 8388608
  997.4 14.6 %slice-start.3 = ((s8[8716288]{0:T(1024)(128)(4,1)}), s8[4194304]{0:T(1024)(128)(4,1)S(1)}, s32[]{:S(2)}) async-start(s8[8716288]{0:T(1024)(128)(4,1)} %bitcast.213), calls=%async_computation.12 | async-start | bytes 8388608
  1006.0 6.1 slice-start.4
  1012.1 3.5 copy-start.1
  (17 other events, 24.8 us)
Sparse Core Ops, SparseCore 0:
  48.1 73.0 all-reduce.7
  154.2 44.6 all-reduce.9
  201.4 64.7 all-reduce.11
  288.6 52.3 all-reduce.13
  345.0 646.9 all-reduce.15
where the time goes:
time: 1030 us; the launch traced here: 1020 us
  waiting for transfers between devices  511 us (50%)
  blocking collectives  281 us (27%)
  matrix products  85.3 us (8%)
  local copies, waits for them, and re-layouts  54.4 us (5%)
  other arithmetic  42 us (4%)
  starting transfers between devices  33.3 us (3%)
  between operations  16 us (2%)
    psum x1, waiting for transfers between devices, on_device(): lax.psum((statistics, grad_gain_attn, grad_w_query, grad_b_query, grad_w_...  331 us
    psum x1, blocking collectives, on_device(): lax.psum((statistics, grad_gain_attn, grad_w_query, grad_b_query, grad_w_...  281 us
    psum x1, waiting for transfers between devices, on_device(): lax.psum(dot_right(grad_gate, w_gate) + dot_right(grad_up, w_up), 'tensor')  67.2 us
    psum x1, waiting for transfers between devices, on_device(): lax.psum(jnp.dot(mixed, w_out, preferred_element_type=jnp.float32), 'tens...  65.8 us
    unnamed x158, local copies, waits for them, and re-layouts  40.9 us
    dot_general x7, matrix products, dot_left(): lax.dot_general(matrix, other, (((0,), (0,)), ((), ())), preferred_elemen...  27.9 us
    dot_general x7, matrix products, dot_right(): lax.dot_general(matrix, other, (((1,), (1,)), ((), ())), preferred_elemen...  25.9 us
    psum x1, waiting for transfers between devices, on_device(): lax.psum((dot_right(grad_q_lin, w_query) + dot_right(grad_k_lin, w_key) +...  22.4 us
  transfers between devices with their start and end apart: 9, of which 6 were waited for; matrix products, arithmetic and copies ran while one was open for 10% of the time, Pallas kernels for 0%

commit v1 on v0

--- a/solution.py
+++ b/solution.py
@@ -74,7 +74,12 @@
 ):
     restore = jnp.argsort(deal_order)
     arrived = (
-        lax.all_to_all(tokens[deal_order], "dp", split_axis=0, concat_axis=1, tiled=True),
+        jnp.concatenate(
+            lax.all_to_all(
+                jnp.stack(jnp.split(tokens[deal_order], lax.axis_size("dp"), axis=0)), "dp", 0, 0
+            ),
+            axis=1,
+        ),
         lax.all_to_all(cotangent[deal_order], "dp", split_axis=0, concat_axis=1, tiled=True),
     )
     stream = arrived[0][0].astype(jnp.float32)

time: 1030 us -> 1070 us (1.039)
  local copies, waits for them, and re-layouts: 54.4 us -> 92 us
    unnamed x158 -> x221, local copies, waits for them, and re-layouts: 40.9 us -> 78.8 us
where the time goes in v1:
time: 1070 us; the launch traced here: 1060 us
  waiting for transfers between devices  511 us (48%)
  blocking collectives  281 us (26%)
  local copies, waits for them, and re-layouts  92 us (9%)
  matrix products  85.3 us (8%)
  other arithmetic  42 us (4%)
  starting transfers between devices  33.3 us (3%)
  between operations  16 us (1%)
    psum x1, waiting for transfers between devices, on_device(): lax.psum((statistics, grad_gain_attn, grad_w_query, grad_b_query, grad_w_...  331 us
    psum x1, blocking collectives, on_device(): lax.psum((statistics, grad_gain_attn, grad_w_query, grad_b_query, grad_w_...  281 us
    unnamed x221, local copies, waits for them, and re-layouts  78.8 us
    psum x1, waiting for transfers between devices, on_device(): lax.psum(dot_right(grad_gate, w_gate) + dot_right(grad_up, w_up), 'tensor')  67.2 us
    psum x1, waiting for transfers between devices, on_device(): lax.psum(jnp.dot(mixed, w_out, preferred_element_type=jnp.float32), 'tens...  65.8 us
    dot_general x7, matrix products, dot_left(): lax.dot_general(matrix, other, (((0,), (0,)), ((), ())), preferred_elemen...  27.8 us
    dot_general x7, matrix products, dot_right(): lax.dot_general(matrix, other, (((1,), (1,)), ((), ())), preferred_elemen...  25.9 us
    psum x1, waiting for transfers between devices, on_device(): lax.psum((dot_right(grad_q_lin, w_query) + dot_right(grad_k_lin, w_key) +...  22.4 us
  transfers between devices with their start and end apart: 9, of which 6 were waited for; matrix products, arithmetic and copies ran while one was open for 10% of the time, Pallas kernels for 0%

profile of v1, /device:TPU:0, one launch (start us, length us, event | category | flops | bytes accessed | tf_op | source)
XLA Modules:
  0.0 1060.2 jit_solution(10512626835295975462)
XLA Ops:
  47.6 10.1 all-to-all-start
  59.6 14.5 %all-to-all-done = bf16[64,1,8,896]{3,2,1,0:T(8,128)(2,1)S(1)} async-done(((bf16[64,1,8,896]{3,2,1,0:T(8,128)(2,1)}), bf16[64,1,8,896]{3,2,1,0:T(8,128)(2,1)S(1)}, u32[]{:S(2)}, u32[]{:S(2)}) %all-to-all-start) | async-done | bytes 917536 | tf_op jit(solution)/shard_map/all_to_all | solution.py:78
  75.4 0.8 convolution_add_fusion.1
  76.3 1.3 fusion.6
  77.7 1.5 fusion.4
  79.8 0.8 copy-done.2
  80.6 2.3 fusion.36
  82.9 0.7 copy-done.8
  83.6 2.0 fusion.103
  85.6 1.6 gather_fusion.2
  87.2 5.5 all-to-all-start.2
  93.0 65.8 %all-reduce.8.cloned.1.call-done = f32[512,896]{1,0:T(8,128)} async-done(((f32[512,896]{1,0:T(8,128)}), f32[512,896]{1,0:T(8,128)}) %all-reduce.8.cloned.1.call-update) | async-done | bytes 1835024 | tf_op jit(solution)/shard_map/psum | solution.py:127
  158.8 1.8 multiply_reduce_fusion.3
  162.1 7.2 fusion.104
  169.3 4.5 fusion.105
  173.8 10.4 multiply_convert_fusion
  184.2 1.5 copy-done.61
  185.7 6.0 convolution_convert_fusion
  191.8 6.0 fusion.106
  197.8 6.4 convolution_add_fusion
  204.6 0.7 log_add_fusion
  205.4 8.2 fusion.108
  213.6 6.1 fusion.109
  219.7 7.5 fusion.65
  227.3 9.3 all-reduce.10.cloned.1.call-done
  236.6 67.2 %all-reduce.12.cloned.1.call-done = f32[512,896]{1,0:T(8,128)} async-done(((f32[512,896]{1,0:T(8,128)}), f32[512,896]{1,0:T(8,128)}) %all-reduce.12.cloned.1.call-update) | async-done | bytes 1835024 | tf_op jit(solution)/shard_map/psum | solution.py:157
  303.8 5.5 select_reduce_fusion
  309.4 2.5 fusion.35
  312.8 2.4 fusion
  315.3 2.4 fusion.7
  317.7 0.7 convolution_bitcast_fusion
  318.5 1.2 convolution_bitcast_fusion.1
  319.7 2.3 convert_reduce_fusion.1
  322.4 0.8 copy-done.15
  324.7 1.4 add_convert_fusion
  326.4 1.1 fusion.61
  327.5 1.1 fusion.63
  328.6 1.9 fusion.59
  330.5 1.8 fusion.56
  332.4 3.8 copy.64
  336.7 8.1 reduce.6
  344.8 2.9 reshape.425
  347.7 8.4 all-to-all-start.1
  356.2 22.4 %all-reduce.14.cloned.1.call-done = bf16[512,896]{1,0:T(8,128)(2,1)} async-done(((bf16[512,896]{1,0:T(8,128)(2,1)}), bf16[512,896]{1,0:T(8,128)(2,1)}) %all-reduce.14.cloned.1.call-update) | async-done | bytes 917520 | tf_op jit(solution)/shard_map/psum | solution.py:200
  378.6 2.0 fusion.29
  380.6 1.7 fusion.55
  382.3 1.4 copy.63
  383.8 6.2 reduce.7
  390.0 1.3 reshape.427
  391.3 8.3 all-to-all-start.3
  400.3 2.0 sort.17
  403.2 2.1 pad_maximum_fusion.3
  405.3 5.4 reshape.426
  410.7 1.0 copy.62
  411.7 2.8 gather_fusion.1
  414.5 280.9 %all-reduce = (f32[896]{0:T(1024)}, f32[448]{0:T(512)}, f32[64]{0:T(128)}, f32[64]{0:T(128)}, f32[896]{0:T(1024)}, /*index=5*/f32[3]{0:T(128)S(1)}) all-reduce(f32[896]{0:T(1024)S(1)} %get-tuple-element.20, f32[448]{0:T(512)S(1)} %reduce_sum.145, f32[64]{0:T(128)S(1)} %convert_reduce_fusion.2, ...), channel_id=1, replica_groups=mesh['dp'=64,'tensor'=2] {'dp'}, use_global_device_ids=true, to_apply=%region_13.14 | all-reduce | flops 2371 | bytes 18968 | tf_op jit(solution)/shard_map/psum | solution.py:229
  696.8 1.6 gather_fusion.3
  698.4 331.3 %all-reduce.16.cloned.1.call-done = (f32[896,448]{0,1:T(8,128)}, f32[896,64]{0,1:T(8,128)}, f32[896,64]{0,1:T(8,128)}, f32[448,896]{1,0:T(8,128)}, f32[896,2432]...) async-done(((f32[896,448]{0,1:T(8,128)}, f32[896,64]{0,1:T(8,128)}, f32[896,64]{0,1:T(8,128)}, f32[448,896]{1,0:T(8,128)}, f32[896,2432]{1,0:T(8,128)}, ...) | async-done | bytes 29818896 | tf_op jit(solution)/shard_map/psum | solution.py:229
  1029.7 2.8 copy.139
  1033.9 1.2 copy.142
  1035.0 8.6 copy.143
  1043.7 4.4 copy.144
  1048.1 1.6 slice-done.3
  1049.8 3.5 copy.145
  (263 shorter events, 53.6 us)
Async XLA Ops:
  8.4 49.4 %copy-start.56 = (bf16[64]{0:T(256)(128)(2,1)S(1)}, bf16[64]{0:T(256)(128)(2,1)}, u32[]{:S(2)}) copy-start(bf16[64]{0:T(256)(128)(2,1)} %param.26) | copy-start | bytes 388
  8.4 49.4 %copy-start.53 = (bf16[896]{0:T(1024)(128)(2,1)S(1)}, bf16[896]{0:T(1024)(128)(2,1)}, u32[]{:S(2)}) copy-start(bf16[896]{0:T(1024)(128)(2,1)} %param.20) | copy-start | bytes 5380
  8.4 49.4 %copy-start.55 = (bf16[448]{0:T(512)(128)(2,1)S(1)}, bf16[448]{0:T(512)(128)(2,1)}, u32[]{:S(2)}) copy-start(bf16[448]{0:T(512)(128)(2,1)} %param.22) | copy-start | bytes 2692
  8.4 49.5 %copy-start.57 = (bf16[64]{0:T(256)(128)(2,1)S(1)}, bf16[64]{0:T(256)(128)(2,1)}, u32[]{:S(2)}) copy-start(bf16[64]{0:T(256)(128)(2,1)} %param.24) | copy-start | bytes 388
  8.4 49.5 %copy-start.58 = (s32[64]{0:T(128)S(1)}, s32[64]{0:T(128)}, u32[]{:S(2)}) copy-start(s32[64]{0:T(128)} %param.18) | copy-start | bytes 772
  12.7 61.8 %copy-start.26 = (bf16[896,64]{0,1:T(8,128)(2,1)S(1)}, bf16[896,64]{0,1:T(8,128)(2,1)}, u32[]{:S(2)}) copy-start(bf16[896,64]{0,1:T(8,128)(2,1)} %param.23) | copy-start | bytes 344068
  47.6 27.7 %copy-start.14 = (bf16[896,448]{0,1:T(8,128)(2,1)S(1)}, bf16[896,448]{0,1:T(8,128)(2,1)}, u32[]{:S(2)}) copy-start(bf16[896,448]{0,1:T(8,128)(2,1)} %param.21) | copy-start | bytes 2408452
  47.6 26.5 %all-to-all-start = ((bf16[64,1,8,896]{3,2,1,0:T(8,128)(2,1)}), bf16[64,1,8,896]{3,2,1,0:T(8,128)(2,1)S(1)}, u32[]{:S(2)}, u32[]{:S(2)}) async-start(bf16[64,1,8,896]{3,2,1,0:T(8,128)(2,1)} %constant_dynamic-update-slice_fusion), calls=%async_computation | async-start | bytes 1835008 | tf_op jit(solution)/shard_map/all_to_all | solution.py:78
  57.7 101.1 %all-reduce.8.cloned.1.call-start = ((), (), s32[]{:S(2)}) async-start(), calls=%async_computation.4 | async-start | bytes 3670016 | tf_op jit(solution)/shard_map/psum | solution.py:127
  57.8 21.4 %copy-start.38 = (f32[896]{0:T(1024)}, f32[896]{0:T(1024)S(1)}, u32[]{:S(2)}) copy-start(f32[896]{0:T(1024)S(1)} %convert_element_type.240) | copy-start | bytes 10756
  58.5 17.7 %copy-start.48 = (f32[32]{0:T(128)}, f32[32]{0:T(128)S(1)}, u32[]{:S(2)}) copy-start(f32[32]{0:T(128)S(1)} %multiply_power_fusion) | copy-start | bytes 388
  59.1 114.7 %copy-start.50 = (pred[512]{0:T(512)(128)(4,1)}, pred[512]{0:T(512)(128)(4,1)S(1)}, u32[]{:S(2)}) copy-start(pred[512]{0:T(512)(128)(4,1)S(1)} %iota_compare_fusion.1) | copy-start | bytes 1540
  59.2 17.0 %copy-start.42 = (f32[512]{0:T(512)}, f32[512]{0:T(512)S(1)}, u32[]{:S(2)}) copy-start(f32[512]{0:T(512)S(1)} %iota_convert_fusion) | copy-start | bytes 6148
  59.5 16.7 %copy-start.16 = (f32[512,32]{0,1:T(8,128)}, f32[512,32]{0,1:T(8,128)S(1)}, u32[]{:S(2)}) copy-start(f32[512,32]{0,1:T(8,128)S(1)} %get-tuple-element.58) | copy-start | bytes 196612
  74.5 4.7 copy-start.44
  75.4 2.3 copy-start.22
  75.4 2.3 copy-start.24
  77.7 2.9 copy-start.2
  77.7 2.9 copy-start.34
  79.3 3.6 copy-start.36
  80.6 3.1 copy-start.6
  82.9 2.7 copy-start.11
  85.6 7.4 copy-start.54
  87.2 86.6 %all-to-all-start.2 = ((bf16[64,8,896]{2,1,0:T(8,128)(2,1)}), bf16[64,8,896]{2,1,0:T(8,128)(2,1)}, u32[]{:S(2)}, u32[]{:S(2)}) async-start(bf16[64,8,896]{2,1,0:T(8,128)(2,1)} %gather_fusion.2), calls=%async_computation.2 | async-start | bytes 1835008 | tf_op jit(solution)/shard_map/all_to_all | solution.py:83
  92.7 143.9 %all-reduce.10.cloned.1.call-start = ((), (), s32[]{:S(2)}) async-start(), calls=%async_computation.5 | async-start | bytes 1835008 | tf_op jit(solution)/shard_map/psum | solution.py:136
  93.0 69.1 %copy-start.32 = (f32[896]{0:T(1024)}, f32[896]{0:T(1024)S(1)}, u32[]{:S(2)}) copy-start(f32[896]{0:T(1024)S(1)} %convert_element_type.253) | copy-start | bytes 10756
  160.6 143.2 %copy-start.3 = (f32[512,896]{1,0:T(8,128)}, f32[512,896]{1,0:T(8,128)S(1)}, u32[]{:S(2)}) copy-start(f32[512,896]{1,0:T(8,128)S(1)} %get-tuple-element.40) | copy-start | bytes 5505028
  161.9 7.5 slice-start.5
  162.1 7.2 copy-start.12
  162.1 7.2 slice-start.6
  191.7 112.1 %all-reduce.12.cloned.1.call-start = ((), (), s32[]{:S(2)}) async-start(), calls=%async_computation.6 | async-start | bytes 3670016 | tf_op jit(solution)/shard_map/psum | solution.py:157
  191.8 6.0 copy-start.63
  204.1 174.5 %all-reduce.14.cloned.1.call-start = ((), (), s32[]{:S(2)}) async-start(), calls=%async_computation.7 | async-start | bytes 1835008 | tf_op jit(solution)/shard_map/psum | solution.py:200
  205.3 8.3 copy-start.13
  205.3 8.3 copy-start.64
  213.6 6.1 copy-start.51
  213.6 6.1 copy-start.62
  303.8 5.6 copy-start.5
  303.8 5.6 copy-start.33
  303.8 5.6 copy-start.41
  303.8 5.6 copy-start.47
  303.8 5.6 copy-start.52
  303.8 8.8 slice-start
  309.4 2.5 copy-start.7
  309.4 3.2 slice-start.1
  315.3 2.4 copy-start.23
  315.3 2.4 copy-start.25
  319.7 2.3 copy-start.17
  326.1 703.6 %all-reduce.16.cloned.1.call-start = ((), (), s32[]{:S(2)}) async-start(), calls=%async_computation.8 | async-start | bytes 59637760 | tf_op jit(solution)/shard_map/psum | solution.py:229
  327.5 3.0 copy-start.9
  344.8 11.3 %copy-start.45 = (f32[512]{0:T(512)S(1)}, f32[512]{0:T(512)}, u32[]{:S(2)}) copy-start(f32[512]{0:T(512)} %copy-done.44) | copy-start | bytes 6148
  347.7 43.6 %all-to-all-start.1 = ((bf16[64,2,3584]{2,1,0:T(2,128)(2,1)}), bf16[64,2,3584]{2,1,0:T(2,128)(2,1)}, u32[]{:S(2)}, u32[]{:S(2)}) async-start(bf16[64,2,3584]{2,1,0:T(2,128)(2,1)} %reshape.425), calls=%async_computation.1 | async-start | bytes 1835008 | tf_op jit(solution)/shard_map/all_to_all | solution.py:248
  390.0 9.6 copy-start.59
  390.0 10.3 copy-start.60
  391.3 304.6 %all-to-all-start.3 = ((bf16[64,2,3584]{2,1,0:T(2,128)(2,1)}), bf16[64,2,3584]{2,1,0:T(2,128)(2,1)S(1)}, u32[]{:S(2)}, u32[]{:S(2)}) async-start(bf16[64,2,3584]{2,1,0:T(2,128)(2,1)} %reshape.427), calls=%async_computation.3 | async-start | bytes 1835008 | tf_op jit(solution)/shard_map/all_to_all | solution.py:251
  410.7 3.8 copy-start.46
  1029.7 2.8 copy-start.21
  1029.7 3.5 copy-start.20
  1029.7 4.2 copy-start.10
  1035.0 8.6 copy-start.4
  1035.0 13.0 %slice-start.2 = ((s8[8716288]{0:T(1024)(128)(4,1)}), s8[4194304]{0:T(1024)(128)(4,1)S(1)}, s32[]{:S(2)}) async-start(s8[8716288]{0:T(1024)(128)(4,1)} %bitcast.469), calls=%async_computation.11 | async-start | bytes 8388608
  1035.0 14.6 %slice-start.3 = ((s8[8716288]{0:T(1024)(128)(4,1)}), s8[4194304]{0:T(1024)(128)(4,1)S(1)}, s32[]{:S(2)}) async-start(s8[8716288]{0:T(1024)(128)(4,1)} %bitcast.469), calls=%async_computation.12 | async-start | bytes 8388608
  1043.7 6.1 slice-start.4
  1049.8 3.5 copy-start.1
  (17 other events, 24.8 us)
Sparse Core Ops, SparseCore 0:
  85.7 73.0 all-reduce.7
  191.8 44.6 all-reduce.9
  239.0 64.7 all-reduce.11
  326.2 52.3 all-reduce.13
  382.7 646.9 all-reduce.15
